TPU v7x, 256 devices: a whole 4x4x8 slice. The times are simulated.
256 devices in a mesh: seq: 32 (over z, y), mp: 4 (over x), req: 2 (over core).
Axes of the slice: x: 4, y: 4, z: 8, core: 2. Of those that a mesh axis runs over, the one named last changes fastest.
Arguments:
- hidden: bfloat16 [2, 8192, 3072], P('req', 'seq', 'mp'), may hold values from -6 to 6
- norm_gain: bfloat16 [3072], replicated, may hold values from 0.5 to 1.5
- w_query: bfloat16 [3072, 1024], P(None, 'mp'), may hold values from -0.109375 to 0.109375
- w_keyval: bfloat16 [3072, 512], P(None, 'mp'), may hold values from -0.109375 to 0.109375
- w_attn_out: bfloat16 [1024, 3072], P('mp'), may hold values from -1.5 to 1.5
- w_inner: bfloat16 [3072, 2, 1536], P(None, None, 'mp'), may hold values from -0.109375 to 0.109375
- w_bc: bfloat16 [3072, 512], P(None, 'mp'), may hold values from -0.109375 to 0.109375
- w_dt: bfloat16 [3072, 12], P(None, 'mp'), may hold values from -0.109375 to 0.109375
- dt_bias: float32 [12], P('mp'), may hold values from -4 to 0
- a_log: float32 [12], P('mp'), may hold values from -12 to 0
- d_skip: float32 [12], P('mp'), may hold values from 0.1 to 10
- conv_x: bfloat16 [4, 1536], P(None, 'mp'), may hold values from -3 to 3
- conv_bc: bfloat16 [4, 512], replicated, may hold values from -3 to 3
- mamba_gain: bfloat16 [1536], P('mp'), may hold values from 0.5 to 1.5
- w_mamba_out: bfloat16 [1536, 3072], P('mp'), may hold values from -0.15625 to 0.15625
- cache: bfloat16 [2, 8192, 512], P('req', 'seq', 'mp'), may hold values from -70 to 70, as said below
- cache_len: int32 [2], P('req'), may hold values from 256 to 8192
- tail_x: bfloat16 [2, 3, 1536], P('req', None, 'mp'), may hold values from -6 to 6
- tail_bc: bfloat16 [2, 3, 512], P('req'), may hold values from -6 to 6
- ssm_init: float32 [2, 12, 128, 256], P('req', 'mp'), may hold values from -6 to 6
Outputs:
- layer_out: bfloat16 [2, 8192, 3072], P('req', 'seq', 'mp')
- new_keyval: bfloat16 [2, 8192, 512], P('req', 'seq', 'mp')
- block_states: float32 [2, 32, 12, 128, 256], P('req', 'seq', 'mp')
Inputs may be any that keep to these rules, and one draw needn't show every extreme that they name: Rows of the cache at or past cache_len are unused.
All inputs are finite; a program needn't handle non-finite values.
Results may differ from a plain program's by a relative error of at most 0.0097.
Values may be sent and summed in bfloat16 or wider, within the bound.
A program may use at most 192 MiB of HBM per device.

v0:
```python
import jax
import jax.numpy as jnp
from jax import lax
from jax.sharding import PartitionSpec as P

HD = 128
QH = 8
KVH = 2
NS = 256
CONV = 4
epsilon = 1e-05
rope_base = 100000000000.0
negative = -1e30


def shifted(block, axis, distance):
    devices = range(lax.axis_size(axis))
    route = [(i - distance, i) for i in devices if i - distance in devices]
    return lax.ppermute(block, axis, route)


def prefix(part, axis, combine, identity):
    place = lax.axis_index(axis)
    gathered = jax.tree.map(lambda a: lax.all_gather(a, axis), part)
    state = jax.tree.map(lambda a, e: jnp.zeros_like(a) + jnp.asarray(e, a.dtype), part, identity)

    def one(turn, state):
        return combine(
            state, jax.tree.map(lambda a: lax.dynamic_index_in_dim(a, turn, 0, False), gathered)
        )

    return lax.fori_loop(0, place, one, state)


def rotate(values, positions):
    half = HD // 2
    freqs = rope_base ** (-jnp.arange(half, dtype=jnp.float32) * 2.0 / HD)
    angles = positions.astype(jnp.float32)[:, None] * freqs[None, :]
    cosine = jnp.cos(angles)[:, None, :]
    sine = jnp.sin(angles)[:, None, :]
    first = values[..., :half]
    second = values[..., half:]
    return jnp.concatenate(
        [first * cosine - second * sine, second * cosine + first * sine], axis=-1
    )


def rms_scale(values):
    mean_sq = jnp.mean(values * values, axis=-1, keepdims=True)
    return values * lax.rsqrt(mean_sq + epsilon)


def causal_conv(tail, inputs, taps):
    padded = jnp.concatenate([tail, inputs], axis=0).astype(jnp.float32)
    count = inputs.shape[0]
    total = jnp.zeros(inputs.shape, jnp.float32)
    for offset in range(CONV):
        total = total + taps[offset].astype(jnp.float32)[None, :] * padded[offset : offset + count]
    return jax.nn.silu(total)


def join_states(earlier, later):
    return (earlier[0] * later[0], later[0][:, None, None] * earlier[1] + later[1])


def shards(
    hidden,
    norm_gain,
    w_query,
    w_keyval,
    w_attn_out,
    w_inner,
    w_bc,
    w_dt,
    dt_bias,
    a_log,
    d_skip,
    conv_x,
    conv_bc,
    mamba_gain,
    w_mamba_out,
    cache,
    cache_len,
    tail_x,
    tail_bc,
    ssm_init,
):
    high = lax.Precision.HIGHEST
    own_rows = hidden[0]
    tokens = own_rows.shape[0]
    seq_pos = lax.axis_index("seq")
    mp_pos = lax.axis_index("mp")
    length = cache_len[0]
    whole = lax.all_gather(own_rows, "mp", axis=1, tiled=True)
    normed = (rms_scale(whole.astype(jnp.float32)) * norm_gain.astype(jnp.float32)).astype(
        jnp.bfloat16
    )
    positions = length + seq_pos * tokens + jnp.arange(tokens, dtype=jnp.int32)
    local_heads = w_query.shape[1] // HD
    query = rotate(
        jnp.dot(normed, w_query, preferred_element_type=jnp.float32).reshape(
            tokens, local_heads, HD
        ),
        positions,
    ).astype(jnp.bfloat16)
    projected = jnp.dot(normed, w_keyval, preferred_element_type=jnp.float32)
    roped = rotate(projected[:, None, :], positions)[:, 0, :]
    kv_block = jnp.where(mp_pos % 2 == 0, roped, projected).astype(jnp.bfloat16)
    bc_block = jnp.dot(normed, w_bc, preferred_element_type=jnp.float32).astype(jnp.bfloat16)
    bc_all = lax.all_gather(bc_block, "mp", axis=1, tiled=True)
    mp_size = lax.axis_size("mp")
    pairs_of = [(i, i ^ 1) for i in range(mp_size)]
    is_key_block = mp_pos % 2 == 0

    def paired(own):
        other = lax.ppermute(own, "mp", pairs_of)
        return jnp.where(
            is_key_block,
            jnp.concatenate([own, other], axis=1),
            jnp.concatenate([other, own], axis=1),
        )

    cache_all = lax.all_gather(paired(cache[0]), "seq", axis=0, tiled=True)
    new_all = lax.all_gather(paired(kv_block), "seq", axis=0, tiled=True)
    inner = jnp.einsum("td,dkc->tkc", normed, w_inner, preferred_element_type=jnp.float32).astype(
        jnp.bfloat16
    )
    rim = CONV - 1
    prev_x, prev_bc = shifted((inner[tokens - rim :, 1], bc_all[tokens - rim :]), "seq", 1)
    first_block = seq_pos == 0
    prev_x = jnp.where(first_block, tail_x[0], prev_x)
    prev_bc = jnp.where(first_block, tail_bc[0], prev_bc)
    mamba_heads = dt_bias.shape[0]
    x_conv = causal_conv(prev_x, inner[:, 1], conv_x).reshape(tokens, mamba_heads, HD)
    bc_conv = causal_conv(prev_bc, bc_all, conv_bc)
    b_mat = bc_conv[:, :NS]
    c_mat = bc_conv[:, NS:]
    step_size = jax.nn.softplus(jnp.dot(normed, w_dt, preferred_element_type=jnp.float32) + dt_bias)
    log_decay = -step_size * jnp.exp(a_log)[None, :]
    cumulative = jnp.cumsum(log_decay, axis=0)
    pairs = jnp.dot(c_mat, b_mat.T, precision=high)
    gap = cumulative[:, None, :] - cumulative[None, :, :]
    token_ids = jnp.arange(tokens)
    lower = (token_ids[:, None] >= token_ids[None, :])[:, :, None]
    decay = jnp.where(lower, jnp.exp(jnp.where(lower, gap, 0.0)), 0.0)
    mixing = decay * pairs[:, :, None] * step_size[None, :, :]
    inner_out = jnp.einsum("tsh,shp->thp", mixing, x_conv, precision=high)
    to_end = jnp.exp(cumulative[-1][None, :] - cumulative) * step_size
    own_state = jnp.einsum("sh,shp,sn->hpn", to_end, x_conv, b_mat, precision=high)
    block_decay = jnp.exp(cumulative[-1])
    seq_size = lax.axis_size("seq")
    rows = HD // seq_size
    pieces = jnp.transpose(own_state.reshape(mamba_heads, seq_size, rows, NS), (1, 0, 2, 3))
    decays = jnp.broadcast_to(block_decay[None, :, None, None], (seq_size, mamba_heads, 1, NS))
    columns = lax.all_to_all(jnp.concatenate([pieces, decays], axis=2), "seq", 0, 0, tiled=True)
    carry = lax.dynamic_slice_in_dim(ssm_init[0], seq_pos * rows, rows, 1)
    entering = []
    for source in range(seq_size):
        entering.append(carry)
        part = columns[source]
        carry = part[:, rows:, :] * carry + part[:, :rows, :]
    entering = lax.all_to_all(jnp.stack(entering, axis=0), "seq", 0, 0, tiled=True)
    incoming = jnp.transpose(entering, (1, 0, 2, 3)).reshape(mamba_heads, HD, NS)
    carried = jnp.exp(cumulative)[:, :, None] * jnp.einsum(
        "tn,hpn->thp", c_mat, incoming, precision=high
    )
    mamba_y = inner_out + carried + d_skip[None, :, None] * x_conv
    state_after = block_decay[:, None, None] * incoming + own_state
    gated = mamba_y * jax.nn.silu(inner[:, 0].astype(jnp.float32).reshape(tokens, mamba_heads, HD))
    mixed = (
        rms_scale(gated).reshape(tokens, mamba_heads * HD) * mamba_gain.astype(jnp.float32)
    ).astype(jnp.bfloat16)
    cache_rows = cache.shape[1]
    shard_rows = cache_rows + tokens
    group = mp_pos * local_heads // (QH // KVH)
    query_index = seq_pos * tokens + jnp.arange(tokens, dtype=jnp.int32)
    scale = 1.0 / float(HD) ** 0.5
    piece = jnp.concatenate([cache_all, new_all], axis=0)
    top = jnp.full((local_heads, tokens), negative, jnp.float32)
    total_cache = cache_all.shape[0]
    index = jnp.arange(piece.shape[0], dtype=jnp.int32)
    in_cache = index < total_cache
    slot_ok = in_cache & (index < length)
    new_index = index - total_cache
    valid = slot_ok[None, :] | (~in_cache)[None, :] & (new_index[None, :] <= query_index[:, None])
    scores = (
        jnp.einsum("qhd,kd->hqk", query, piece[:, :HD], preferred_element_type=jnp.float32) * scale
    )
    masked = jnp.where(valid[None], scores, negative)
    new_top = jnp.maximum(top, jnp.max(masked, axis=-1))
    weights = jnp.where(valid[None], jnp.exp(masked - new_top[:, :, None]), 0.0)
    total = jnp.sum(weights, axis=-1)
    accum = jnp.einsum(
        "hqk,kd->hqd",
        weights.astype(jnp.bfloat16),
        piece[:, HD : 2 * HD],
        preferred_element_type=jnp.float32,
    )
    top, total, accum = (new_top, total, accum)
    attended = jnp.transpose(accum / total[:, :, None], (1, 0, 2)).reshape(tokens, local_heads * HD)
    attended = attended.astype(jnp.bfloat16)
    term = jnp.dot(attended, w_attn_out, preferred_element_type=jnp.float32)
    term = term + jnp.dot(mixed, w_mamba_out, preferred_element_type=jnp.float32)
    summed = lax.psum_scatter(term, "mp", scatter_dimension=1, tiled=True)
    layer = (summed + own_rows.astype(jnp.float32)).astype(jnp.bfloat16)
    return (layer[None], kv_block[None], state_after[None, None])


def solution(mesh):
    placed = (
        P("req", "seq", "mp"),
        P(),
        P(None, "mp"),
        P(None, "mp"),
        P("mp", None),
        P(None, None, "mp"),
        P(None, "mp"),
        P(None, "mp"),
        P("mp"),
        P("mp"),
        P("mp"),
        P(None, "mp"),
        P(),
        P("mp"),
        P("mp", None),
        P("req", "seq", "mp"),
        P("req"),
        P("req", None, "mp"),
        P("req", None, None),
        P("req", "mp", None, None),
    )
    return jax.shard_map(
        shards,
        mesh=mesh,
        in_specs=placed,
        out_specs=(P("req", "seq", "mp"), P("req", "seq", "mp"), P("req", "seq", "mp", None, None)),
        check_vma=False,
    )
```

profile of v0, /device:TPU:1, one launch (start us, length us, event | category | flops | bytes accessed | tf_op | source)
XLA Modules:
  0.0 330.6 jit_solution(8155268910153722102)
XLA Ops:
  8.0 0.9 copy.66
  8.9 2.1 collective-permute-start
  14.5 0.9 convert_reduce_fusion.3
  15.4 0.8 slice_convert_fusion.4
  16.8 1.3 multiply_cosine_fusion
  18.8 15.6 %and_or_fusion = pred[256,16384]{0,1:T(8,128)(4,1)} fusion(s32[256]{0:T(256)S(1)} %iota_add_fusion.1, s32[16384]{0:T(1024)S(1)} %iota_add_fusion, pred[16384]{0:T(1024)(128)(4,1)S(1)} %get-tuple-element.103, pred[16384]{0:T(1024)(128)(4,1)S(1)} %get-tuple-element.104), kind=kLoop, calls=%fused_computation.7 | loop fusion | flops 12582912 | bytes 4293632 | tf_op jit(solution)/shard_map/or | solution.py:185
  34.4 8.3 %all-gather.9.cloned.1.call-done = bf16[1,256,3072]{2,1,0:T(8,128)(2,1)} async-done(((bf16[1,256,768]{2,1,0:T(8,128)(2,1)}), bf16[1,256,3072]{2,1,0:T(8,128)(2,1)}) %all-gather.9.cloned.1.call-update) | async-done | bytes 1572880 | tf_op jit(solution)/shard_map/all_gather | solution.py:94
  42.7 1.8 fusion.9
  44.5 1.9 fusion.11
  46.4 1.1 copy-done.1
  48.1 0.9 reduce-window.6
  49.5 4.3 %fusion.13 = bf16[256,2,384]{2,0,1:T(8,128)(2,1)S(1)} fusion(bf16[3072,2,384]{2,1,0:T(2,128)(2,1)} %param.25, bf16[256,3072]{1,0:T(8,128)(2,1)} %copy-done.1), kind=kOutput, calls=%fused_computation.20 | convolution fusion | flops 1208156160 | bytes 6684672 | tf_op jit(solution)/shard_map/td,dkc->tkc/dot_general | solution.py:125
  53.9 3.1 collective-permute-start.2
  58.6 9.8 %all_gather.15 = bf16[256,512]{1,0:T(8,128)(2,1)S(1)} all-gather(bf16[256,128]{1,0:T(8,128)(2,1)S(1)} %convolution_convert_fusion), channel_id=1, replica_groups=mesh['seq'=32,'mp'=4,'req'=2] {'mp'}, dimensions={1}, use_global_device_ids=true | all-gather | bytes 327680 | tf_op jit(solution)/shard_map/all_gather | solution.py:110
  68.4 2.7 collective-permute-start.3
  71.5 0.9 copy.72
  72.8 1.5 fusion.45
  74.7 1.0 pad_maximum_fusion
  75.7 10.7 %all-to-all-start = ((f32[32,3,5,256]{3,1,2,0:T(4,128)}), f32[32,3,5,256]{3,1,2,0:T(4,128)}, u32[]{:S(2)}, u32[]{:S(2)}) async-start(f32[32,3,5,256]{3,1,2,0:T(4,128)} %pad_maximum_fusion), calls=%async_computation | async-start | bytes 1310720 | tf_op jit(solution)/shard_map/all_to_all | solution.py:155
  86.5 2.3 fusion.90
  89.1 1.0 collective-permute-start.1
  90.8 1.5 collective-permute-done.1
  93.0 8.7 %all-to-all-done = f32[32,3,5,256]{3,1,2,0:T(4,128)} async-done(((f32[32,3,5,256]{3,1,2,0:T(4,128)}), f32[32,3,5,256]{3,1,2,0:T(4,128)}, u32[]{:S(2)}, u32[]{:S(2)}) %all-to-all-start) | async-done | bytes 491552 | tf_op jit(solution)/shard_map/all_to_all | solution.py:155
  101.8 0.9 slice_bitcast_fusion.30
  102.8 1.0 slice_bitcast_fusion.11
  122.8 1.9 copy.77
  124.7 7.0 %all-to-all-start.1 = ((f32[32,3,4,256]{3,2,1,0:T(4,128)}), f32[32,3,4,256]{3,2,1,0:T(4,128)}, u32[]{:S(2)}, u32[]{:S(2)}) async-start(f32[32,3,4,256]{3,2,1,0:T(4,128)} %copy.77), calls=%async_computation.1 | async-start | bytes 786432 | tf_op jit(solution)/shard_map/all_to_all | solution.py:162
  132.0 2.6 fusion.91
  135.3 1.0 copy.86
  136.3 1.9 copy.79
  138.2 1.7 copy.85
  140.0 1.8 subtract_convert_fusion
  142.2 1.4 all-to-all-done.1
  143.6 1.8 copy.78
  145.3 1.9 reshape.277
  147.2 1.5 convolution_multiply_fusion
  148.7 2.5 multiply_reduce_fusion
  151.4 4.6 %constant_dynamic-update-slice_fusion.1 = bf16[16384,256]{0,1:T(8,128)(2,1)} fusion(bf16[8192,256]{0,1:T(8,128)(2,1)} %all-gather.5.cloned.1.call-done), kind=kLoop, calls=%fused_computation.102 | loop fusion | bytes 8388608
  156.0 62.0 %all-gather.7.cloned.1.call-done = bf16[8192,256]{0,1:T(8,128)(2,1)} async-done(((bf16[256,256]{0,1:T(8,128)(2,1)}), bf16[8192,256]{0,1:T(8,128)(2,1)}) %all-gather.7.cloned.1.call-update) | async-done | bytes 4194320 | tf_op jit(solution)/shard_map/all_gather | solution.py:124
  218.0 4.6 %constant_dynamic-update-slice_fusion = bf16[16384,256]{0,1:T(8,128)(2,1)} fusion(bf16[16384,256]{0,1:T(8,128)(2,1)} %constant_dynamic-update-slice_fusion.1, bf16[8192,256]{0,1:T(8,128)(2,1)} %all-gather.7.cloned.1.call-done), kind=kLoop, calls=%fused_computation.101 | loop fusion | bytes 8388608 | tf_op jit(solution)/shard_map/concatenate | solution.py:178
  222.6 17.3 %fusion = (f32[2,256]{1,0:T(2,128)S(1)}, f32[16384,256,2]{1,0,2:T(8,128)}) fusion(pred[256,16384]{0,1:T(8,128)(4,1)} %and_or_fusion, bf16[256,2,64]{2,0,1:T(8,128)(2,1)S(1)} %copy-done.8, bf16[256,2,64]{2,0,1:T(8,128)(2,1)S(1)} %copy-done.7, bf16[16384,256]{0,1:T(8,128)(2,1)} %constant_dynamic-update-slice_fusion), kind=kOutput, calls=%fused_computation.2 | convolution fusion | flops 2172911104 | bytes 42076160 | tf_op jit(solution)/shard_map/qhd,kd->hqk/dot_general | solution.py:187
  239.9 15.7 %fusion.1 = f32[2,256]{1,0:T(2,128)S(1)} fusion(f32[16384,256,2]{1,0,2:T(8,128)} %get-tuple-element.98, f32[2,256]{1,0:T(2,128)S(1)} %broadcast_maximum_fusion, pred[256,16384]{0,1:T(8,128)(4,1)} %and_or_fusion), kind=kLoop, calls=%fused_computation.3 | loop fusion | flops 41942528 | bytes 37752832 | tf_op jit(solution)/shard_map/reduce_sum | solution.py:192
  255.6 17.2 %fusion.27 = bf16[256,2,128]{0,2,1:T(8,128)(2,1)S(1)} fusion(f32[16384,256,2]{1,0,2:T(8,128)} %get-tuple-element.98, f32[2,256]{1,0:T(2,128)S(1)} %broadcast_maximum_fusion, pred[256,16384]{0,1:T(8,128)(4,1)} %and_or_fusion, bf16[16384,256]{0,1:T(8,128)(2,1)} %constant_dynamic-update-slice_fusion, f32[256,2]{0,1:T(2,128)S(1)} %bitcast.367), kind=kOutput, calls=%fused_computation.30 | convolution fusion | flops 2189557760 | bytes 42078208 | tf_op jit(solution)/shard_map/hqk,kd->hqd/dot_general | solution.py:193
  272.8 2.0 fusion.92
  274.9 2.7 convolution_add_fusion
  278.4 0.9 add_bitcast_fusion
  279.2 42.8 %reduce-scatter.2.cloned.1.call-done = f32[256,768]{1,0:T(8,128)} async-done(((f32[256,3072]{1,0:T(8,128)}), f32[256,768]{1,0:T(8,128)}) %reduce-scatter.2.cloned.1.call-update) | async-done | bytes 786448 | tf_op jit(solution)/shard_map/reduce_scatter | solution.py:204
  322.0 2.0 fusion.40
  (135 shorter events, 31.5 us)
Async XLA Ops:
  7.2 267.7 %copy-start = (bf16[384,3072]{1,0:T(8,128)(2,1)S(1)}, bf16[384,3072]{1,0:T(8,128)(2,1)}, u32[]{:S(2)}) copy-start(bf16[384,3072]{1,0:T(8,128)(2,1)} %param.34) | copy-start | bytes 7077892
  7.2 35.5 %all-gather.9.cloned.1.call-start = ((), (), s32[]{:S(2)}) async-start(), calls=%async_computation.6 | async-start | bytes 1966080 | tf_op jit(solution)/shard_map/all_gather | solution.py:94
  7.9 143.5 %all-gather.5.cloned.1.call-start = ((), (), s32[]{:S(2)}) async-start(), calls=%async_computation.3 | async-start | bytes 4325376 | tf_op jit(solution)/shard_map/all_gather | solution.py:123
  8.9 9.2 %collective-permute-start = (bf16[256,128]{0,1:T(8,128)(2,1)S(1)}, bf16[256,128]{0,1:T(8,128)(2,1)S(1)}, u32[]{:S(2)}, u32[]{:S(2)}) collective-permute-start(bf16[256,128]{0,1:T(8,128)(2,1)S(1)} %bitcast.357), channel_id=1, source_target_pairs={{0,2},{2,0},{4,6},{6,4},{1,3},{3,1},{5,7},{7,5},{8,10},{10,8},{12,... | collective-permute-start | bytes 196616 | tf_op jit(solution)/shard_map/ppermute | solution.py:116
  18.8 28.8 %copy-start.9 = (bf16[3072,3]{0,1:T(4,128)(2,1)S(1)}, bf16[3072,3]{0,1:T(4,128)(2,1)}, u32[]{:S(2)}) copy-start(bf16[3072,3]{0,1:T(4,128)(2,1)} %param.27) | copy-start | bytes 55300
  18.8 28.8 %copy-start.14 = (f32[3]{0:T(128)S(1)}, f32[3]{0:T(128)}, u32[]{:S(2)}) copy-start(f32[3]{0:T(128)} %param.28) | copy-start | bytes 40
  46.4 1.2 copy-start.1
  49.5 8.6 %copy-start.2 = (bf16[256,3072]{1,0:T(8,128)(2,1)S(1)}, bf16[256,3072]{1,0:T(8,128)(2,1)}, u32[]{:S(2)}) copy-start(bf16[256,3072]{1,0:T(8,128)(2,1)} %copy-done.1) | copy-start | bytes 4718596
  49.5 8.6 %copy-start.4 = (bf16[3072,128]{1,0:T(8,128)(2,1)S(1)}, bf16[3072,128]{1,0:T(8,128)(2,1)}, u32[]{:S(2)}) copy-start(bf16[3072,128]{1,0:T(8,128)(2,1)} %param.26) | copy-start | bytes 2359300
  49.5 21.7 %copy-start.11 = (bf16[1,3,384]{2,1,0:T(4,128)(2,1)S(1)}, bf16[1,3,384]{2,1,0:T(4,128)(2,1)}, u32[]{:S(2)}) copy-start(bf16[1,3,384]{2,1,0:T(4,128)(2,1)} %param.37) | copy-start | bytes 6916
  53.8 18.6 %copy-start.10 = (bf16[1,3,512]{2,1,0:T(4,128)(2,1)S(1)}, bf16[1,3,512]{2,1,0:T(4,128)(2,1)}, u32[]{:S(2)}) copy-start(bf16[1,3,512]{2,1,0:T(4,128)(2,1)} %param.38) | copy-start | bytes 9220
  53.9 17.3 %collective-permute-start.2 = (bf16[3,384]{1,0:T(4,128)(2,1)S(1)}, bf16[3,384]{1,0:T(4,128)(2,1)S(1)}, u32[]{:S(2)}, u32[]{:S(2)}) collective-permute-start(bf16[3,384]{1,0:T(4,128)(2,1)S(1)} %slice_bitcast_fusion.73), channel_id=1, source_target_pairs={{0,8},{8,16},{16,24},{24,32},{32,40},{40,48},{48,56},{56,64},{64,7... | collective-permute-start | bytes 6920 | tf_op jit(solution)/shard_map/ppermute | solution.py:19
  68.4 6.2 %copy-start.12 = (f32[3]{0:T(128)}, f32[3]{0:T(128)S(1)}, u32[]{:S(2)}) copy-start(f32[3]{0:T(128)S(1)} %exp.54) | copy-start | bytes 40
  68.4 4.0 %collective-permute-start.3 = (bf16[3,512]{1,0:T(4,128)(2,1)S(1)}, bf16[3,512]{1,0:T(4,128)(2,1)S(1)}, u32[]{:S(2)}, u32[]{:S(2)}) collective-permute-start(bf16[3,512]{1,0:T(4,128)(2,1)S(1)} %slice.510), channel_id=1, source_target_pairs={{0,8},{8,16},{16,24},{24,32},{32,40},{40,48},{48,56},{56,64},{64,7... | collective-permute-start | bytes 9224 | tf_op jit(solution)/shard_map/ppermute | solution.py:19
  75.7 26.1 %all-to-all-start = ((f32[32,3,5,256]{3,1,2,0:T(4,128)}), f32[32,3,5,256]{3,1,2,0:T(4,128)}, u32[]{:S(2)}, u32[]{:S(2)}) async-start(f32[32,3,5,256]{3,1,2,0:T(4,128)} %pad_maximum_fusion), calls=%async_computation | async-start | bytes 1310720 | tf_op jit(solution)/shard_map/all_to_all | solution.py:155
  86.4 131.6 %all-gather.7.cloned.1.call-start = ((), (), s32[]{:S(2)}) async-start(), calls=%async_computation.4 | async-start | bytes 4325376 | tf_op jit(solution)/shard_map/all_gather | solution.py:124
  89.1 3.2 copy-start.5
  89.1 3.2 collective-permute-start.1
  124.7 18.9 %all-to-all-start.1 = ((f32[32,3,4,256]{3,2,1,0:T(4,128)}), f32[32,3,4,256]{3,2,1,0:T(4,128)}, u32[]{:S(2)}, u32[]{:S(2)}) async-start(f32[32,3,4,256]{3,2,1,0:T(4,128)} %copy.77), calls=%async_computation.1 | async-start | bytes 786432 | tf_op jit(solution)/shard_map/all_to_all | solution.py:162
  131.7 190.3 %reduce-scatter.2.cloned.1.call-start = ((), (), s32[]{:S(2)}) async-start(), calls=%async_computation.5 | async-start | bytes 3932160 | tf_op jit(solution)/shard_map/reduce_scatter | solution.py:204
  156.0 66.6 %copy-start.7 = (bf16[256,2,64]{2,0,1:T(8,128)(2,1)S(1)}, bf16[256,2,64]{2,0,1:T(8,128)(2,1)}, u32[]{:S(2)}) copy-start(bf16[256,2,64]{2,0,1:T(8,128)(2,1)} %get-tuple-element.49) | copy-start | bytes 196612
  156.0 66.6 %copy-start.8 = (bf16[256,2,64]{2,0,1:T(8,128)(2,1)S(1)}, bf16[256,2,64]{2,0,1:T(8,128)(2,1)}, u32[]{:S(2)}) copy-start(bf16[256,2,64]{2,0,1:T(8,128)(2,1)} %get-tuple-element.50) | copy-start | bytes 196612
  274.9 2.8 copy-start.6
  274.9 3.5 %copy-start.3 = (f32[3,128,256]{2,1,0:T(8,128)S(1)}, f32[3,128,256]{2,1,0:T(8,128)}, u32[]{:S(2)}) copy-start(f32[3,128,256]{2,1,0:T(8,128)} %reshape.277) | copy-start | bytes 1179652
  274.9 3.5 %copy-start.13 = (f32[3]{0:T(128)S(1)}, f32[3]{0:T(128)}, u32[]{:S(2)}) copy-start(f32[3]{0:T(128)} %copy-done.12) | copy-start | bytes 40
Sparse Core Ops, SparseCore 0:
  9.8 32.8 all-gather.8
  45.2 86.1 all-gather.4
  133.8 84.1 all-gather.6
  277.7 44.2 reduce-scatter.1
where the time goes:
time: 332 us; the launch traced here: 331 us
  waiting for transfers between devices  125 us (38%)
  other arithmetic  69.1 us (21%)
  matrix products  55.4 us (17%)
  local copies, waits for them, and re-layouts  28.8 us (9%)
  starting transfers between devices  27.1 us (8%)
  between operations  14.9 us (4%)
  blocking collectives  9.8 us (3%)
    all_gather x1, waiting for transfers between devices, shards(): new_all = lax.all_gather(paired(kv_block), 'seq', axis=0, tiled=True)  62 us
    reduce_scatter x1, waiting for transfers between devices, shards(): summed = lax.psum_scatter(term, 'mp', scatter_dimension=1, tiled=True)  42.8 us
    unnamed x31, other arithmetic  18.3 us
    dot_general x1, matrix products, shards(): jnp.einsum('qhd,kd->hqk', query, piece[:, :HD], preferred_element_type=jn...  17.3 us
    dot_general x1, matrix products, shards(): jnp.einsum('hqk,kd->hqd', weights.astype(jnp.bfloat16), piece[:, HD:2 * H...  17.2 us
    reduce_sum x1, other arithmetic, shards(): total = jnp.sum(weights, axis=-1)  15.7 us
    or x1, other arithmetic, shards(): slot_ok[None, :]  15.6 us
    unnamed x37, local copies, waits for them, and re-layouts  10.8 us
  transfers between devices with their start and end apart: 10, of which 6 were waited for; matrix products, arithmetic and copies ran while one was open for 27% of the time, Pallas kernels for 0%

commit v1 on v0

--- a/solution.py
+++ b/solution.py
@@ -11,6 +11,27 @@
 epsilon = 1e-05
 rope_base = 100000000000.0
 negative = -1e30
+
+
+def collect(x, axis, dim):
+    size, position, rows = (lax.axis_size(axis), lax.axis_index(axis), x.shape[dim])
+    ahead = [(i, (i + 1) % size) for i in range(size)]
+    left = [(i, (i - 1) % size) for i in range(size)]
+    out = jnp.zeros((*x.shape[:dim], size * rows, *x.shape[dim + 1 :]), x.dtype)
+    out = lax.dynamic_update_slice_in_dim(out, x, position * rows, axis=dim)
+    from_left = from_right = x
+    half = size // 2
+    for lap in range(1, half + 1):
+        from_left = lax.ppermute(from_left, axis, ahead)
+        out = lax.dynamic_update_slice_in_dim(
+            out, from_left, (position - lap) % size * rows, axis=dim
+        )
+        if lap < size - half:
+            from_right = lax.ppermute(from_right, axis, left)
+            out = lax.dynamic_update_slice_in_dim(
+                out, from_right, (position + lap) % size * rows, axis=dim
+            )
+    return out
 
 
 def shifted(block, axis, distance):
@@ -91,7 +112,7 @@
     seq_pos = lax.axis_index("seq")
     mp_pos = lax.axis_index("mp")
     length = cache_len[0]
-    whole = lax.all_gather(own_rows, "mp", axis=1, tiled=True)
+    whole = collect(own_rows, "mp", 1)
     normed = (rms_scale(whole.astype(jnp.float32)) * norm_gain.astype(jnp.float32)).astype(
         jnp.bfloat16
     )

time: 332 us -> 317 us (0.955)
  waiting for transfers between devices: 125 us -> 85.6 us
  other arithmetic: 69.1 us -> 81.6 us
  local copies, waits for them, and re-layouts: 28.8 us -> 34.7 us
  starting transfers between devices: 27.1 us -> 32.5 us
    all_gather x1, waiting for transfers between devices: 62 us -> 24.1 us  [shards(): new_all = lax.all_gather(paired(kv_block), 'seq', axis=0, tiled=True)]
    all_gather x1 -> x0, waiting for transfers between devices: 8.26 us -> none  [shards(): whole = lax.all_gather(own_rows, 'mp', axis=1, tiled=True)]
    or x1, other arithmetic: 15.6 us -> 22.6 us  [shards(): slot_ok[None, :]]
    ppermute x2, waiting for transfers between devices: 1.52 us -> 7.87 us  [paired(): other = lax.ppermute(own, 'mp', pairs_of)]
    ppermute x0 -> x3, starting transfers between devices: none -> 3.86 us  [the longest x2 2.5 us: collect(): from_left = lax.ppermute(from_left, axis, ahead)]
    unnamed x37 -> x73, local copies, waits for them, and re-layouts: 10.8 us -> 11.6 us
  transfers between devices with their start and end apart: 10 -> 12, of which waited for: 6 -> 7; matrix products, arithmetic and copies ran while one was open for 27% -> 35% of each run, Pallas kernels for 0% -> 0%
where the time goes in v1:
time: 317 us; the launch traced here: 316 us
  waiting for transfers between devices  85.6 us (27%)
  other arithmetic  81.6 us (26%)
  matrix products  55.7 us (18%)
  local copies, waits for them, and re-layouts  34.7 us (11%)
  starting transfers between devices  32.5 us (10%)
  between operations  15.2 us (5%)
  blocking collectives  10.3 us (3%)
    reduce_scatter x1, waiting for transfers between devices, shards(): summed = lax.psum_scatter(term, 'mp', scatter_dimension=1, tiled=True)  42.8 us
    all_gather x1, waiting for transfers between devices, shards(): new_all = lax.all_gather(paired(kv_block), 'seq', axis=0, tiled=True)  24.1 us
    or x1, other arithmetic, shards(): slot_ok[None, :]  22.6 us
    unnamed x31, other arithmetic  18.3 us
    dot_general x1, matrix products, shards(): jnp.einsum('qhd,kd->hqk', query, piece[:, :HD], preferred_element_type=jn...  17.5 us
    dot_general x1, matrix products, shards(): jnp.einsum('hqk,kd->hqd', weights.astype(jnp.bfloat16), piece[:, HD:2 * H...  17.2 us
    reduce_sum x1, other arithmetic, shards(): total = jnp.sum(weights, axis=-1)  15.6 us
    all_to_all x1, starting transfers between devices, shards(): lax.all_to_all(jnp.concatenate([pieces, decays], axis=2), 'seq', 0, 0, ti...  12.7 us
  transfers between devices with their start and end apart: 12, of which 7 were waited for; matrix products, arithmetic and copies ran while one was open for 35% of the time, Pallas kernels for 0%

profile of v1, /device:TPU:1, one launch (start us, length us, event | category | flops | bytes accessed | tf_op | source)
XLA Modules:
  0.0 315.6 jit_solution(10771457005133139884)
XLA Ops:
  7.2 2.1 collective-permute-start.1
  9.4 1.4 collective-permute-start.2
  10.7 1.6 copy.66
  14.9 5.4 %collective-permute-done = bf16[256,128]{0,1:T(8,128)(2,1)} collective-permute-done((bf16[256,128]{0,1:T(8,128)(2,1)}, bf16[256,128]{0,1:T(8,128)(2,1)}, u32[]{:S(2)}, u32[]{:S(2)}) %collective-permute-start) | collective-permute-done | bytes 65568 | tf_op jit(solution)/shard_map/ppermute | solution.py:137
  20.3 1.6 maximum_select_fusion
  21.9 22.6 %and_or_fusion = pred[256,16384]{0,1:T(8,128)(4,1)} fusion(s32[256]{0:T(256)} %iota_add_fusion.1, s32[16384]{0:T(1024)} %iota_add_fusion, pred[16384]{0:T(1024)(128)(4,1)S(1)} %get-tuple-element.103, pred[16384]{0:T(1024)(128)(4,1)} %get-tuple-element.104), kind=kLoop, calls=%fused_computation.7 | loop fusion | flops 12582912 | bytes 4293632 | tf_op jit(solution)/shard_map/or | solution.py:206
  45.3 1.2 multiply_cosine_fusion
  47.2 1.4 broadcast_in_dim.47
  49.7 1.4 slice_convert_fusion.4
  51.2 1.2 exp.48
  52.4 1.2 convert_element_type.91
  53.6 1.3 convert_element_type.78
  54.9 1.4 convert_reduce_fusion.3
  59.7 1.8 fusion.9
  61.5 1.9 fusion.11
  63.4 1.2 copy-done.1
  66.5 4.3 %fusion.13 = bf16[256,2,384]{2,0,1:T(8,128)(2,1)S(1)} fusion(bf16[3072,2,384]{2,1,0:T(2,128)(2,1)} %param.25, bf16[256,3072]{1,0:T(8,128)(2,1)} %copy-done.1), kind=kOutput, calls=%fused_computation.20 | convolution fusion | flops 1208156160 | bytes 6684672 | tf_op jit(solution)/shard_map/td,dkc->tkc/dot_general | solution.py:146
  70.9 3.9 %collective-permute-start.5 = (bf16[3,384]{1,0:T(4,128)(2,1)S(1)}, bf16[3,384]{1,0:T(4,128)(2,1)S(1)}, u32[]{:S(2)}, u32[]{:S(2)}) collective-permute-start(bf16[3,384]{1,0:T(4,128)(2,1)S(1)} %slice_bitcast_fusion.73), channel_id=1, source_target_pairs={{0,8},{8,16},{16,24},{24,32},{32,40},{40,48},{48,56},{56,64},{64,7... | collective-permute-start | bytes 6920 | tf_op jit(solution)/shard_map/ppermute | solution.py:40
  77.0 10.3 %all_gather.11 = bf16[256,512]{1,0:T(8,128)(2,1)S(1)} all-gather(bf16[256,128]{1,0:T(8,128)(2,1)S(1)} %convolution_convert_fusion), channel_id=1, replica_groups=mesh['seq'=32,'mp'=4,'req'=2] {'mp'}, dimensions={1}, use_global_device_ids=true | all-gather | bytes 327680 | tf_op jit(solution)/shard_map/all_gather | solution.py:131
  87.3 2.5 collective-permute-start.6
  91.7 1.5 fusion.44
  94.5 12.7 %all-to-all-start = ((f32[32,3,5,256]{3,1,2,0:T(4,128)}), f32[32,3,5,256]{3,1,2,0:T(4,128)}, u32[]{:S(2)}, u32[]{:S(2)}) async-start(f32[32,3,5,256]{3,1,2,0:T(4,128)} %pad_maximum_fusion), calls=%async_computation | async-start | bytes 1310720 | tf_op jit(solution)/shard_map/all_to_all | solution.py:176
  107.3 2.3 fusion.89
  110.9 2.4 collective-permute-done.4
  114.1 8.0 %all-to-all-done = f32[32,3,5,256]{3,1,2,0:T(4,128)} async-done(((f32[32,3,5,256]{3,1,2,0:T(4,128)}), f32[32,3,5,256]{3,1,2,0:T(4,128)}, u32[]{:S(2)}, u32[]{:S(2)}) %all-to-all-start) | async-done | bytes 491552 | tf_op jit(solution)/shard_map/all_to_all | solution.py:176
  129.1 1.0 slice_bitcast_fusion.11
  143.0 1.9 copy.77
  144.9 9.1 %all-to-all-start.1 = ((f32[32,3,4,256]{3,2,1,0:T(4,128)}), f32[32,3,4,256]{3,2,1,0:T(4,128)}, u32[]{:S(2)}, u32[]{:S(2)}) async-start(f32[32,3,4,256]{3,2,1,0:T(4,128)} %copy.77), calls=%async_computation.1 | async-start | bytes 786432 | tf_op jit(solution)/shard_map/all_to_all | solution.py:183
  154.1 2.6 fusion.90
  157.4 1.0 copy.86
  158.4 1.9 copy.79
  160.3 1.7 copy.85
  162.1 1.8 subtract_convert_fusion
  164.3 1.9 all-to-all-done.1
  166.3 1.8 copy.78
  168.0 1.9 reshape.277
  169.9 1.5 convolution_multiply_fusion
  171.4 2.6 multiply_reduce_fusion
  174.2 4.6 %constant_dynamic-update-slice_fusion.1 = bf16[16384,256]{0,1:T(8,128)(2,1)} fusion(bf16[8192,256]{0,1:T(8,128)(2,1)} %all-gather.3.cloned.1.call-done), kind=kLoop, calls=%fused_computation.101 | loop fusion | bytes 8388608
  178.8 24.1 %all-gather.5.cloned.1.call-done = bf16[8192,256]{0,1:T(8,128)(2,1)} async-done(((bf16[256,256]{0,1:T(8,128)(2,1)}), bf16[8192,256]{0,1:T(8,128)(2,1)}) %all-gather.5.cloned.1.call-update) | async-done | bytes 4194320 | tf_op jit(solution)/shard_map/all_gather | solution.py:145
  202.9 4.6 %constant_dynamic-update-slice_fusion = bf16[16384,256]{0,1:T(8,128)(2,1)} fusion(bf16[16384,256]{0,1:T(8,128)(2,1)} %constant_dynamic-update-slice_fusion.1, bf16[8192,256]{0,1:T(8,128)(2,1)} %all-gather.5.cloned.1.call-done), kind=kLoop, calls=%fused_computation.100 | loop fusion | bytes 8388608 | tf_op jit(solution)/shard_map/concatenate | solution.py:199
  207.5 17.5 %fusion = (f32[2,256]{1,0:T(2,128)S(1)}, f32[16384,256,2]{1,0,2:T(8,128)}) fusion(pred[256,16384]{0,1:T(8,128)(4,1)} %and_or_fusion, bf16[256,2,64]{2,0,1:T(8,128)(2,1)S(1)} %copy-done.9, bf16[256,2,64]{2,0,1:T(8,128)(2,1)S(1)} %copy-done.8, bf16[16384,256]{0,1:T(8,128)(2,1)} %constant_dynamic-update-slice_fusion), kind=kOutput, calls=%fused_computation.2 | convolution fusion | flops 2172911104 | bytes 42076160 | tf_op jit(solution)/shard_map/qhd,kd->hqk/dot_general | solution.py:208
  225.0 15.6 %fusion.1 = f32[2,256]{1,0:T(2,128)S(1)} fusion(f32[16384,256,2]{1,0,2:T(8,128)} %get-tuple-element.98, f32[2,256]{1,0:T(2,128)S(1)} %broadcast_maximum_fusion, pred[256,16384]{0,1:T(8,128)(4,1)} %and_or_fusion), kind=kLoop, calls=%fused_computation.3 | loop fusion | flops 41942528 | bytes 37752832 | tf_op jit(solution)/shard_map/reduce_sum | solution.py:213
  240.6 17.2 %fusion.27 = bf16[256,2,128]{0,2,1:T(8,128)(2,1)S(1)} fusion(f32[16384,256,2]{1,0,2:T(8,128)} %get-tuple-element.98, f32[2,256]{1,0:T(2,128)S(1)} %broadcast_maximum_fusion, pred[256,16384]{0,1:T(8,128)(4,1)} %and_or_fusion, bf16[16384,256]{0,1:T(8,128)(2,1)} %constant_dynamic-update-slice_fusion, f32[256,2]{0,1:T(2,128)S(1)} %bitcast.365), kind=kOutput, calls=%fused_computation.30 | convolution fusion | flops 2189557760 | bytes 42078208 | tf_op jit(solution)/shard_map/hqk,kd->hqd/dot_general | solution.py:214
  257.9 2.0 fusion.91
  259.9 2.7 convolution_add_fusion
  264.2 42.8 %reduce-scatter.2.cloned.1.call-done = f32[256,768]{1,0:T(8,128)} async-done(((f32[256,3072]{1,0:T(8,128)}), f32[256,768]{1,0:T(8,128)}) %reduce-scatter.2.cloned.1.call-update) | async-done | bytes 786448 | tf_op jit(solution)/shard_map/reduce_scatter | solution.py:225
  307.0 2.0 fusion.39
  (179 shorter events, 39.9 us)
Async XLA Ops:
  7.2 252.7 %copy-start = (bf16[384,3072]{1,0:T(8,128)(2,1)S(1)}, bf16[384,3072]{1,0:T(8,128)(2,1)}, u32[]{:S(2)}) copy-start(bf16[384,3072]{1,0:T(8,128)(2,1)} %param.34) | copy-start | bytes 7077892
  7.2 41.4 %copy-start.4 = (bf16[1,256,768]{2,1,0:T(8,128)(2,1)S(1)}, bf16[1,256,768]{2,1,0:T(8,128)(2,1)}, u32[]{:S(2)}) copy-start(bf16[1,256,768]{2,1,0:T(8,128)(2,1)} %param.20) | copy-start | bytes 1179652
  7.2 167.0 %all-gather.3.cloned.1.call-start = ((), (), s32[]{:S(2)}) async-start(), calls=%async_computation.3 | async-start | bytes 4325376 | tf_op jit(solution)/shard_map/all_gather | solution.py:144
  7.2 42.1 %collective-permute-start.1 = (bf16[256,768]{1,0:T(8,128)(2,1)}, bf16[256,768]{1,0:T(8,128)(2,1)S(1)}, u32[]{:S(2)}, u32[]{:S(2)}) collective-permute-start(bf16[256,768]{1,0:T(8,128)(2,1)} %bitcast.349), channel_id=1, source_target_pairs={{0,2},{2,4},{4,6},{6,0},{1,3},{3,5},{5,7},{7,1},{8,10},{10,12},{12... | collective-permute-start | bytes 1179656 | tf_op jit(solution)/shard_map/ppermute | solution.py:25
  9.4 47.8 %collective-permute-start.2 = (bf16[256,768]{1,0:T(8,128)(2,1)}, bf16[256,768]{1,0:T(8,128)(2,1)S(1)}, u32[]{:S(2)}, u32[]{:S(2)}) collective-permute-start(bf16[256,768]{1,0:T(8,128)(2,1)} %bitcast.350), channel_id=1, source_target_pairs={{0,6},{2,0},{4,2},{6,4},{1,7},{3,1},{5,3},{7,5},{8,14},{10,8},{12,... | collective-permute-start | bytes 1179656 | tf_op jit(solution)/shard_map/ppermute | solution.py:30
  12.3 8.0 %collective-permute-start = (bf16[256,128]{0,1:T(8,128)(2,1)}, bf16[256,128]{0,1:T(8,128)(2,1)}, u32[]{:S(2)}, u32[]{:S(2)}) collective-permute-start(bf16[256,128]{0,1:T(8,128)(2,1)} %bitcast.355), channel_id=1, source_target_pairs={{0,2},{2,0},{4,6},{6,4},{1,3},{3,1},{5,7},{7,5},{8,10},{10,8},{12,... | collective-permute-start | bytes 196616 | tf_op jit(solution)/shard_map/ppermute | solution.py:137
  44.5 2.0 copy-start.29
  44.6 0.8 copy-start.22
  48.6 16.0 %copy-start.31 = (f32[3]{0:T(128)S(1)}, f32[3]{0:T(128)}, u32[]{:S(2)}) copy-start(f32[3]{0:T(128)} %param.28) | copy-start | bytes 40
  49.4 9.5 %collective-permute-start.3 = (bf16[256,768]{1,0:T(8,128)(2,1)S(1)}, bf16[256,768]{1,0:T(8,128)(2,1)S(1)}, u32[]{:S(2)}, u32[]{:S(2)}) collective-permute-start(bf16[256,768]{1,0:T(8,128)(2,1)S(1)} %collective-permute-done.1), channel_id=1, source_target_pairs={{0,2},{2,4},{4,6},{6,0},{1,3},{3,5},{5,7},{7,1},{8,10},{10,12},{12... | collective-permute-start | bytes 1179656 | tf_op jit(solution)/shard_map/ppermute | solution.py:25
  54.9 9.7 %copy-start.10 = (bf16[3072,3]{0,1:T(4,128)(2,1)S(1)}, bf16[3072,3]{0,1:T(4,128)(2,1)}, u32[]{:S(2)}) copy-start(bf16[3072,3]{0,1:T(4,128)(2,1)} %param.27) | copy-start | bytes 55300
  54.9 9.7 %copy-start.32 = (f32[3]{0:T(128)S(1)}, f32[3]{0:T(128)}, u32[]{:S(2)}) copy-start(f32[3]{0:T(128)} %exp.48) | copy-start | bytes 40
  63.4 1.2 copy-start.1
  66.4 8.4 %copy-start.11 = (f32[1,3,2,128]{3,1,2,0:T(4,128)}, f32[1,3,2,128]{3,1,2,0:T(4,128)S(1)}, u32[]{:S(2)}) copy-start(f32[1,3,2,128]{3,1,2,0:T(4,128)S(1)} %copy.109) | copy-start | bytes 9220
  66.4 10.0 %copy-start.2 = (bf16[256,3072]{1,0:T(8,128)(2,1)S(1)}, bf16[256,3072]{1,0:T(8,128)(2,1)}, u32[]{:S(2)}) copy-start(bf16[256,3072]{1,0:T(8,128)(2,1)} %copy-done.1) | copy-start | bytes 4718596
  66.4 10.0 %copy-start.5 = (bf16[3072,128]{1,0:T(8,128)(2,1)S(1)}, bf16[3072,128]{1,0:T(8,128)(2,1)}, u32[]{:S(2)}) copy-start(bf16[3072,128]{1,0:T(8,128)(2,1)} %param.26) | copy-start | bytes 2359300
  66.4 23.4 %copy-start.26 = (bf16[1,3,384]{2,1,0:T(4,128)(2,1)S(1)}, bf16[1,3,384]{2,1,0:T(4,128)(2,1)}, u32[]{:S(2)}) copy-start(bf16[1,3,384]{2,1,0:T(4,128)(2,1)} %param.37) | copy-start | bytes 6916
  70.8 19.1 %copy-start.18 = (f32[384]{0:T(512)S(1)}, f32[384]{0:T(512)}, u32[]{:S(2)}) copy-start(f32[384]{0:T(512)} %get-tuple-element.15) | copy-start | bytes 4612
  70.8 19.1 %copy-start.19 = (f32[384]{0:T(512)S(1)}, f32[384]{0:T(512)}, u32[]{:S(2)}) copy-start(f32[384]{0:T(512)} %get-tuple-element.16) | copy-start | bytes 4612
  70.8 19.1 %copy-start.20 = (f32[384]{0:T(512)S(1)}, f32[384]{0:T(512)}, u32[]{:S(2)}) copy-start(f32[384]{0:T(512)} %get-tuple-element.17) | copy-start | bytes 4612
  70.8 19.1 %copy-start.21 = (f32[384]{0:T(512)S(1)}, f32[384]{0:T(512)}, u32[]{:S(2)}) copy-start(f32[384]{0:T(512)} %get-tuple-element.18) | copy-start | bytes 4612
  70.9 20.3 %copy-start.24 = (bf16[1,3,512]{2,1,0:T(4,128)(2,1)S(1)}, bf16[1,3,512]{2,1,0:T(4,128)(2,1)}, u32[]{:S(2)}) copy-start(bf16[1,3,512]{2,1,0:T(4,128)(2,1)} %param.38) | copy-start | bytes 9220
  70.9 20.4 %copy-start.14 = (f32[1,512]{1,0:T(1,128)S(1)}, f32[1,512]{1,0:T(1,128)}, u32[]{:S(2)}) copy-start(f32[1,512]{1,0:T(1,128)} %get-tuple-element.90) | copy-start | bytes 6148
  70.9 20.4 %copy-start.15 = (f32[1,512]{1,0:T(1,128)S(1)}, f32[1,512]{1,0:T(1,128)}, u32[]{:S(2)}) copy-start(f32[1,512]{1,0:T(1,128)} %get-tuple-element.91) | copy-start | bytes 6148
  70.9 20.4 %copy-start.16 = (f32[1,512]{1,0:T(1,128)S(1)}, f32[1,512]{1,0:T(1,128)}, u32[]{:S(2)}) copy-start(f32[1,512]{1,0:T(1,128)} %get-tuple-element.92) | copy-start | bytes 6148
  70.9 20.4 %copy-start.17 = (f32[1,512]{1,0:T(1,128)S(1)}, f32[1,512]{1,0:T(1,128)}, u32[]{:S(2)}) copy-start(f32[1,512]{1,0:T(1,128)} %get-tuple-element.93) | copy-start | bytes 6148
  70.9 18.9 %collective-permute-start.5 = (bf16[3,384]{1,0:T(4,128)(2,1)S(1)}, bf16[3,384]{1,0:T(4,128)(2,1)S(1)}, u32[]{:S(2)}, u32[]{:S(2)}) collective-permute-start(bf16[3,384]{1,0:T(4,128)(2,1)S(1)} %slice_bitcast_fusion.73), channel_id=1, source_target_pairs={{0,8},{8,16},{16,24},{24,32},{32,40},{40,48},{48,56},{56,64},{64,7... | collective-permute-start | bytes 6920 | tf_op jit(solution)/shard_map/ppermute | solution.py:40
  87.3 6.1 %copy-start.27 = (f32[3]{0:T(128)}, f32[3]{0:T(128)S(1)}, u32[]{:S(2)}) copy-start(f32[3]{0:T(128)S(1)} %exp.54) | copy-start | bytes 40
  87.3 3.8 %collective-permute-start.6 = (bf16[3,512]{1,0:T(4,128)(2,1)S(1)}, bf16[3,512]{1,0:T(4,128)(2,1)S(1)}, u32[]{:S(2)}, u32[]{:S(2)}) collective-permute-start(bf16[3,512]{1,0:T(4,128)(2,1)S(1)} %slice.510), channel_id=1, source_target_pairs={{0,8},{8,16},{16,24},{24,32},{32,40},{40,48},{48,56},{56,64},{64,7... | collective-permute-start | bytes 9224 | tf_op jit(solution)/shard_map/ppermute | solution.py:40
  91.6 17.9 %copy-start.23 = (f32[256]{0:T(256)S(1)}, f32[256]{0:T(256)}, u32[]{:S(2)}) copy-start(f32[256]{0:T(256)} %copy-done.22) | copy-start | bytes 3076
  91.6 17.9 %copy-start.30 = (f32[64]{0:T(128)S(1)}, f32[64]{0:T(128)}, u32[]{:S(2)}) copy-start(f32[64]{0:T(128)} %copy-done.29) | copy-start | bytes 772
  94.5 27.5 %all-to-all-start = ((f32[32,3,5,256]{3,1,2,0:T(4,128)}), f32[32,3,5,256]{3,1,2,0:T(4,128)}, u32[]{:S(2)}, u32[]{:S(2)}) async-start(f32[32,3,5,256]{3,1,2,0:T(4,128)} %pad_maximum_fusion), calls=%async_computation | async-start | bytes 1310720 | tf_op jit(solution)/shard_map/all_to_all | solution.py:176
  107.3 95.6 %all-gather.5.cloned.1.call-start = ((), (), s32[]{:S(2)}) async-start(), calls=%async_computation.4 | async-start | bytes 4325376 | tf_op jit(solution)/shard_map/all_gather | solution.py:145
  110.0 3.4 %copy-start.6 = (bf16[256,128]{0,1:T(8,128)(2,1)}, bf16[256,128]{0,1:T(8,128)(2,1)S(1)}, u32[]{:S(2)}) copy-start(bf16[256,128]{0,1:T(8,128)(2,1)S(1)} %fusion.61) | copy-start | bytes 196612
  110.0 3.4 %collective-permute-start.4 = (bf16[256,128]{0,1:T(8,128)(2,1)S(1)}, bf16[256,128]{0,1:T(8,128)(2,1)S(1)}, u32[]{:S(2)}, u32[]{:S(2)}) collective-permute-start(bf16[256,128]{0,1:T(8,128)(2,1)S(1)} %fusion.61), channel_id=1, source_target_pairs={{0,2},{2,0},{4,6},{6,4},{1,3},{3,1},{5,7},{7,5},{8,10},{10,8},{12,... | collective-permute-start | bytes 196616 | tf_op jit(solution)/shard_map/ppermute | solution.py:137
  144.9 21.3 %all-to-all-start.1 = ((f32[32,3,4,256]{3,2,1,0:T(4,128)}), f32[32,3,4,256]{3,2,1,0:T(4,128)}, u32[]{:S(2)}, u32[]{:S(2)}) async-start(f32[32,3,4,256]{3,2,1,0:T(4,128)} %copy.77), calls=%async_computation.1 | async-start | bytes 786432 | tf_op jit(solution)/shard_map/all_to_all | solution.py:183
  154.0 17.4 %copy-start.12 = (f32[1,3,2,128]{3,1,2,0:T(4,128)S(1)}, f32[1,3,2,128]{3,1,2,0:T(4,128)}, u32[]{:S(2)}) copy-start(f32[1,3,2,128]{3,1,2,0:T(4,128)} %copy-done.11) | copy-start | bytes 9220
  154.0 17.4 %copy-start.25 = (f32[256,3]{0,1:T(4,128)S(1)}, f32[256,3]{0,1:T(4,128)}, u32[]{:S(2)}) copy-start(f32[256,3]{0,1:T(4,128)} %get-tuple-element.88) | copy-start | bytes 9220
  154.0 153.0 %reduce-scatter.2.cloned.1.call-start = ((), (), s32[]{:S(2)}) async-start(), calls=%async_computation.5 | async-start | bytes 3932160 | tf_op jit(solution)/shard_map/reduce_scatter | solution.py:225
  163.9 10.2 %copy-start.13 = (f32[384]{0:T(512)S(1)}, f32[384]{0:T(512)}, u32[]{:S(2)}) copy-start(f32[384]{0:T(512)} %convert_element_type.91) | copy-start | bytes 4612
  178.8 28.7 %copy-start.8 = (bf16[256,2,64]{2,0,1:T(8,128)(2,1)S(1)}, bf16[256,2,64]{2,0,1:T(8,128)(2,1)}, u32[]{:S(2)}) copy-start(bf16[256,2,64]{2,0,1:T(8,128)(2,1)} %get-tuple-element.49) | copy-start | bytes 196612
  178.8 28.7 %copy-start.9 = (bf16[256,2,64]{2,0,1:T(8,128)(2,1)S(1)}, bf16[256,2,64]{2,0,1:T(8,128)(2,1)}, u32[]{:S(2)}) copy-start(bf16[256,2,64]{2,0,1:T(8,128)(2,1)} %get-tuple-element.50) | copy-start | bytes 196612
  259.9 2.7 copy-start.7
  259.9 3.5 %copy-start.3 = (f32[3,128,256]{2,1,0:T(8,128)S(1)}, f32[3,128,256]{2,1,0:T(8,128)}, u32[]{:S(2)}) copy-start(f32[3,128,256]{2,1,0:T(8,128)} %reshape.277) | copy-start | bytes 1179652
  259.9 3.5 %copy-start.28 = (f32[3]{0:T(128)S(1)}, f32[3]{0:T(128)}, u32[]{:S(2)}) copy-start(f32[3]{0:T(128)} %copy-done.27) | copy-start | bytes 40
Sparse Core Ops, SparseCore 0:
  22.1 84.3 all-gather.2
  114.2 88.6 all-gather.4
  262.8 44.2 reduce-scatter.1
